TPU v7x, 256 devices: a whole 4x4x8 slice. The times are simulated.
256 devices in a mesh: pair: 32 (over x, z_hi, y), rows: 8 (over z_lo, core).
Axes of the slice: x: 4, y: 4, z: 8 (z_hi: 2, z_lo: 4; z = z_hi * 4 + z_lo), core: 2. Of those that a mesh axis runs over, the one named last changes fastest.
Arguments:
- samples: float32 [32768, 4096], P(('pair', 'rows')), may hold values from -400 to 400
- keep_mask: int32 [256, 8], P(('pair', 'rows')), may hold values 0 or 1
- keep_rate: float32 [8], replicated, may hold values from 0.5 to 1
Outputs:
- cosine: float32 [64, 512, 512], P('pair', 'rows')
All inputs are finite; a program needn't handle non-finite values. No bound on the sum of `keep_mask` on one device may be relied on, other than what follows from the above.
Results may differ from a plain program's by a relative error of at most 0.00005.
Values sent between devices are 32-bit elements; how exact they have to be, the bound alone decides.
A program may use at most 128 MiB of HBM per device.

v0:
```python
import jax
import jax.numpy as jnp
from jax import lax
from jax.sharding import Mesh
from jax.sharding import PartitionSpec as P

BLOCKS = 8
BLOCK_COLS = 512
BLOCK_ROWS = 128
COLS = 4096
PAIR = ("pair_0", "pair_1", "pair_2")
ROWS = ("rows_0", "rows_1")
PAIR_ROWS = ("pair_0", "pair_1", "pair_2", "rows_0", "rows_1")


EPS = 1e-06


def one_axis_at_a_time(value, axes):
    for axis in axes:
        value = lax.psum(value, axis)
    return value


def reduced_to_own(tiles, axes, turns):
    inside = tiles.shape[1:]
    tiles = tiles.reshape(*(lax.axis_size(a) for a in axes), *inside)
    tiles = jnp.moveaxis(tiles, turns, range(len(axes))).reshape(-1, *inside)
    for k in turns:
        tiles = lax.psum_scatter(tiles, axes[k], scatter_dimension=0, tiled=True)
    return tiles[0]


def in_blocks(value, dim, count):
    lengths = value.shape
    tiles = value.reshape(*lengths[:dim], count, lengths[dim] // count, *lengths[dim + 1 :])
    return jnp.moveaxis(tiles, dim, 0)


def scatter_axes(value, axes, turns, dim):
    count = lax.axis_size(axes)
    return reduced_to_own(in_blocks(value, dim, count), axes, turns)


def per_device(samples, keep_mask, keep_rate):
    pair_count = lax.axis_size(PAIR)
    row_count = lax.axis_size(ROWS)
    tile_count = BLOCKS * BLOCKS // pair_count
    pair_index = lax.axis_index(PAIR)
    row_index = lax.axis_index(ROWS)
    local_rows = samples.shape[0]
    slice_rows = BLOCK_COLS // row_count
    squares = jnp.sum(samples * samples, axis=0)
    col_norms = jnp.sqrt(one_axis_at_a_time(squares, PAIR_ROWS) + EPS)
    weights = keep_mask.astype(jnp.float32)
    masked = (
        samples.reshape(local_rows // BLOCK_ROWS, BLOCK_ROWS, BLOCKS, BLOCK_COLS)
        * weights[:, None, :, None]
    )
    masked_rows = masked.reshape(local_rows, COLS)
    initial = jnp.zeros((BLOCKS * BLOCKS, slice_rows, BLOCK_COLS), jnp.float32)
    piece = lax.all_gather(masked_rows, ROWS, axis=0, tiled=True)
    count = piece.shape[0]
    split_cols = piece.reshape(count, BLOCKS, row_count, slice_rows)
    left_cols = lax.dynamic_slice_in_dim(split_cols, row_index, 1, 2)[:, :, 0, :]
    right_cols = piece.reshape(count, BLOCKS, BLOCK_COLS)
    product = jnp.einsum(
        "rai,rbj->abij",
        left_cols,
        right_cols,
        precision=lax.Precision.HIGHEST,
        preferred_element_type=jnp.float32,
    )
    tile_grams = product.reshape(initial.shape)
    summed = scatter_axes(tile_grams, PAIR, (0, 2, 1), 0)
    first_tile = pair_index * tile_count
    left_block = first_tile // BLOCKS
    right_start = first_tile % BLOCKS
    norm_blocks = col_norms.reshape(BLOCKS, BLOCK_COLS)
    row_norms = lax.dynamic_slice(
        norm_blocks, (left_block, row_index * slice_rows), (1, slice_rows)
    )[0]
    col_part = lax.dynamic_slice(norm_blocks, (right_start, jnp.int32(0)), (tile_count, BLOCK_COLS))
    left_rate = lax.dynamic_slice(keep_rate, (left_block,), (1,))
    right_rate = lax.dynamic_slice(keep_rate, (right_start,), (tile_count,))
    row_scale = left_rate * row_norms
    col_scale = right_rate[:, None] * col_part
    return summed / (row_scale[None, :, None] * col_scale[:, None, :])


def solution(mesh):
    finer = Mesh(
        mesh.devices.reshape(4, 2, 4, 4, 2), ("pair_0", "pair_1", "pair_2", "rows_0", "rows_1")
    )
    placed = (P(PAIR_ROWS, None), P(PAIR_ROWS, None), P())
    return jax.shard_map(
        per_device, mesh=finer, in_specs=placed, out_specs=P(PAIR, ROWS, None), check_vma=False
    )
```

profile of v0, /device:TPU:25, one launch (start us, length us, event | category | flops | bytes accessed | tf_op | source)
XLA Modules:
  0.0 414.9 jit_solution(9704003310913359644)
XLA Ops:
  6.5 0.0 copy-start.1
  6.5 0.0 all-gather.2.cloned.1.call-start
  6.5 1.9 copy.6
  8.5 0.0 copy-done.1
  8.5 0.1 broadcast_bitcast_fusion
  8.6 2.0 broadcast_multiply_fusion
  10.5 0.0 all-gather.2.cloned.1.call-update
  10.6 0.0 reduce-scatter.4.cloned.1.call-start
  10.6 175.2 %all-gather.2.cloned.1.call-done = f32[1024,4096]{0,1:T(8,128)} async-done(((f32[128,4096]{0,1:T(8,128)}), f32[1024,4096]{0,1:T(8,128)}) %all-gather.2.cloned.1.call-update) | async-done | bytes 16777232 | tf_op jit(solution)/shard_map/all_gather | solution.py:62
  185.8 30.1 %fusion = f32[8,512,8,64]{1,3,2,0:T(8,128)S(1)} fusion(f32[1024,8,512,1]{0,2,3,1:T(8,128)} %bitcast.30, f32[1024,8,8,64]{0,3,2,1:T(8,128)} %bitcast.31, s32[]{:T(128)S(6)} %select_n.25), kind=kOutput, calls=%fused_computation | convolution fusion | flops 25769803776 | bytes 27262980 | tf_op jit(solution)/shard_map/rai,rbj->abij/dot_general | solution.py:67
  215.9 4.3 %copy.8 = f32[4,4,2,2,64,512]{5,4,3,2,1,0:T(8,128)} copy(f32[4,4,2,2,64,512]{5,4,2,0,3,1:T(8,128)S(1)} %bitcast.28) | data formatting | bytes 16777216 | tf_op jit(solution)/shard_map/transpose | solution.py:28
  220.2 0.0 reduce-scatter.4.cloned.1.call-update
  220.2 0.0 copy-start
  220.2 0.0 reduce-scatter.6.cloned.1.call-start
  220.3 82.1 %reduce-scatter.4.cloned.1.call-done = f32[8,2,64,512]{3,2,1,0:T(8,128)} async-done(((f32[32,2,64,512]{3,2,1,0:T(8,128)}), f32[8,2,64,512]{3,2,1,0:T(8,128)}) %reduce-scatter.4.cloned.1.call-update) | async-done | bytes 2097168 | tf_op jit(solution)/shard_map/reduce_scatter | solution.py:30
  302.4 0.0 copy-start.2
  302.4 0.0 reduce-scatter.6.cloned.1.call-update
  302.4 0.0 reduce-scatter.8.cloned.1.call-start
  302.4 32.7 %reduce-scatter.6.cloned.1.call-done = f32[2,2,64,512]{3,2,1,0:T(8,128)} async-done(((f32[8,2,64,512]{3,2,1,0:T(8,128)}), f32[2,2,64,512]{3,2,1,0:T(8,128)}) %reduce-scatter.6.cloned.1.call-update) | async-done | bytes 524304 | tf_op jit(solution)/shard_map/reduce_scatter | solution.py:30
  335.1 0.0 reduce-scatter.8.cloned.1.call-update
  335.2 0.0 copy-done
  335.2 0.2 multiply_reduce_fusion
  335.4 13.1 %psum.35 = f32[4096]{0:T(1024)S(1)} all-reduce(f32[4096]{0:T(1024)S(1)} %multiply_reduce_fusion), channel_id=1, replica_groups=mesh['pair_0'=4,'pair_1'=2,'pair_2'=4,'rows_0'=4,'rows_1'=2] {'pair_0'}, use_global_device_ids=true, to_apply=%region_4.0 | all-reduce | flops 4096 | bytes 32768 | tf_op jit(solution)/shard_map/psum | solution.py:21
  348.4 18.6 %psum.36 = f32[4096]{0:T(1024)S(1)} all-reduce(f32[4096]{0:T(1024)S(1)} %psum.35), channel_id=1, replica_groups=mesh['pair_0'=4,'pair_1'=2,'pair_2'=4,'rows_0'=4,'rows_1'=2] {'pair_1'}, use_global_device_ids=true, to_apply=%region_5.0 | all-reduce | flops 4096 | bytes 32768 | tf_op jit(solution)/shard_map/psum | solution.py:21
  367.0 11.1 %psum.37 = f32[4096]{0:T(1024)S(1)} all-reduce(f32[4096]{0:T(1024)S(1)} %psum.36), channel_id=1, replica_groups=mesh['pair_0'=4,'pair_1'=2,'pair_2'=4,'rows_0'=4,'rows_1'=2] {'pair_2'}, use_global_device_ids=true, to_apply=%region_6.0 | all-reduce | flops 4096 | bytes 32768 | tf_op jit(solution)/shard_map/psum | solution.py:21
  378.1 12.1 %psum.38 = f32[4096]{0:T(1024)S(1)} all-reduce(f32[4096]{0:T(1024)S(1)} %psum.37), channel_id=1, replica_groups=mesh['pair_0'=4,'pair_1'=2,'pair_2'=4,'rows_0'=4,'rows_1'=2] {'rows_0'}, use_global_device_ids=true, to_apply=%region_7.0 | all-reduce | flops 4096 | bytes 32768 | tf_op jit(solution)/shard_map/psum | solution.py:21
  390.2 14.8 %psum.39 = f32[4096]{0:T(1024)S(1)} all-reduce(f32[4096]{0:T(1024)S(1)} %psum.38), channel_id=1, replica_groups=mesh['pair_0'=4,'pair_1'=2,'pair_2'=4,'rows_0'=4,'rows_1'=2] {'rows_1'}, use_global_device_ids=true, to_apply=%region_8.0 | all-reduce | flops 4096 | bytes 32768 | tf_op jit(solution)/shard_map/psum | solution.py:21
  405.1 0.0 copy-done.2
  405.1 0.1 dynamic_slice.18
  405.2 0.6 dynamic_slice.16
  405.8 0.7 multiply_bitcast_fusion
  406.5 0.1 dynamic-slice_multiply_fusion
  406.6 0.0 reduce-scatter.8.cloned.1.call-done
  406.6 1.8 bitcast_divide_fusion
  (4 shorter events, 0.0 us)
Async XLA Ops:
  6.5 1.9 copy-start.1
  6.5 179.3 %all-gather.2.cloned.1.call-start = ((), (), s32[]{:S(2)}) async-start(), calls=%async_computation.3 | async-start | bytes 18874368 | tf_op jit(solution)/shard_map/all_gather | solution.py:62
  10.6 291.8 %reduce-scatter.4.cloned.1.call-start = ((), (), s32[]{:S(2)}) async-start(), calls=%async_computation.4 | async-start | bytes 10485760 | tf_op jit(solution)/shard_map/reduce_scatter | solution.py:30
  220.2 114.9 %copy-start = (f32[128,4096]{1,0:T(8,128)S(1)}, f32[128,4096]{1,0:T(8,128)}, u32[]{:S(2)}) copy-start(f32[128,4096]{1,0:T(8,128)} %param.3) | copy-start | bytes 6291460
  220.2 114.9 %reduce-scatter.6.cloned.1.call-start = ((), (), s32[]{:S(2)}) async-start(), calls=%async_computation.5 | async-start | bytes 2621440 | tf_op jit(solution)/shard_map/reduce_scatter | solution.py:30
  302.4 102.7 %copy-start.2 = (f32[8]{0:T(128)S(1)}, f32[8]{0:T(128)}, u32[]{:S(2)}) copy-start(f32[8]{0:T(128)} %param.5) | copy-start | bytes 100
  302.4 104.2 %reduce-scatter.8.cloned.1.call-start = ((), (), s32[]{:S(2)}) async-start(), calls=%async_computation.6 | async-start | bytes 786432 | tf_op jit(solution)/shard_map/reduce_scatter | solution.py:30
Sparse Core Ops, SparseCore 0:
  10.7 175.0 all-gather.1
  220.3 81.9 reduce-scatter.3
  304.9 30.1 reduce-scatter.5
  337.5 27.2 reduce-scatter.7
where the time goes:
time: 419 us; the launch traced here: 415 us
  waiting for transfers between devices  290 us (69%)
  blocking collectives  69.7 us (17%)
  matrix products  30.1 us (7%)
  between operations  13.2 us (3%)
  local copies, waits for them, and re-layouts  6.96 us (2%)
  other arithmetic  4.7 us (1%)
    all_gather x1, waiting for transfers between devices, per_device(): piece = lax.all_gather(masked_rows, ROWS, axis=0, tiled=True)  175 us
    reduce_scatter x3, waiting for transfers between devices, reduced_to_own(): tiles = lax.psum_scatter(tiles, axes[k], scatter_dimension=0, tiled=True)  115 us
    psum x5, blocking collectives, one_axis_at_a_time(): value = lax.psum(value, axis)  69.7 us
    dot_general x1, matrix products, per_device(): jnp.einsum('rai,rbj->abij', left_cols, right_cols, precision=lax.Precisio...  30.1 us
  transfers between devices with their start and end apart: 4, of which 3 were waited for; matrix products, arithmetic and copies ran while one was open for 0% of the time, Pallas kernels for 0%

commit v1 on v0

v1 whole, which is shorter than its diff:
```python
import jax
import jax.numpy as jnp
from jax import lax
from jax.experimental import pallas as pl
from jax.experimental.pallas import tpu as pltpu
from jax.sharding import Mesh
from jax.sharding import PartitionSpec as P

AXES = ("x", "zh", "y", "zl", "c")
EPS = 1e-06
MESH = pl.DeviceIdType.MESH
OFFS = (2, 1, 3, 0)
ROWS = 136
F32 = jnp.float32
BF16 = jnp.bfloat16


def kernel(
    a_ref, w_ref, rate_ref, out_ref,
    R, LO, W, LTh, LTl, RH, RL, D, RSQ, YR, YRz, ZRy, ZRz, CF,
    ag_r, ag_s, rel_r, rel_s, two_s, sib_s, lo_r, lo_s, m_r, m_s,
    yr_r, yr_s, yz_r, yz_s, zy_r, zy_s, zz_r, zz_s, f_r, f_s,
):
    x, zh, y, zl, c = (lax.axis_index(a) for a in AXES)
    z = zh * 4 + zl
    oc = 1 - c

    def dev(dx=0, dy=0, dz=0, core=None):
        zz = (z + dz + 8) % 8
        return ((x + dx) % 4, zz // 4, (y + dy) % 4, zz % 4, c if core is None else core)

    pending = []

    def remote(src, dst, ss, rs, to):
        return pltpu.make_async_remote_copy(
            src_ref=src, dst_ref=dst, send_sem=ss, recv_sem=rs, device_id=to, device_id_type=MESH
        )

    def send(src, dst, ss, rs, to):
        copy = remote(src, dst, ss, rs, to)
        copy.start()
        pending.append(copy)

    def arrived(dst, rs, ss):
        remote(dst, dst, ss, rs, dev(core=oc)).wait_recv()

    partners = [dev(dx=d, core=k) for d in (1, 2, 3) for k in (0, 1)] + [dev(core=oc)]
    partners += [dev(dy=1), dev(dy=3), dev(dz=1), dev(dz=7)]
    bar = pltpu.get_barrier_semaphore()
    for p in partners:
        pl.semaphore_signal(bar, inc=1, device_id=p, device_id_type=MESH)
    pl.semaphore_wait(bar, len(partners))

    def cols(q, parity, r):
        start = pl.multiple_of((2 * q + parity) * 512 + r * 256, 256)
        return a_ref.at[:, pl.ds(start, 256)]

    def slot(dx, cs):
        return pl.ds(pl.multiple_of((dx * 2 + cs) * 128, 128), 128)

    def own_send(r, kq):
        for d in (1, 3):
            for k in (0, 1):
                q = (x + d + kq) % 4
                send(cols(q, k, r), R.at[kq, r, slot(4 - d, c), :],
                     ag_s.at[r, d // 2, k, kq], ag_r.at[r, 4 - d, c, kq], dev(dx=d, core=k))

    def sibling_send(r, kq):
        send(cols((x + kq) % 4, oc, r), R.at[kq, r, slot(0, c), :],
             sib_s.at[r, kq], ag_r.at[r, 0, c, kq], dev(core=oc))

    def wait_from(r, dx, cs, kq):
        arrived(R.at[kq, r, slot(dx, cs), :], ag_r.at[r, dx, cs, kq], ag_s.at[0, 0, 0, 0])

    for d in (1, 2, 3):
        for k in (0, 1):
            send(w_ref, W.at[(4 - d) * 2 + c], m_s.at[d * 2 + k], m_r.at[4 - d, c], dev(dx=d, core=k))
    send(w_ref, W.at[c], m_s.at[0], m_r.at[0, c], dev(core=oc))
    for r in (0, 1):
        sibling_send(r, 0)
        own_send(r, 0)
        for k in (0, 1):
            send(cols((x + 2) % 4, k, r), R.at[0, r, slot(2, c), :],
                 two_s.at[r, k], ag_r.at[r, 2, c, 0], dev(dx=2, core=k))
    for kq in (1, 2, 3):
        sibling_send(0, kq)
        own_send(0, kq)
    own_send(1, 1)

    W[c] = w_ref[...]
    for r in (0, 1):
        for kq in range(4):
            start = pl.multiple_of((2 * ((x + kq) % 4) + c) * 512 + r * 256, 256)
            R[kq, r, slot(0, c), :] = a_ref[:, pl.ds(start, 256)]

    def relay(r):
        for kq in (1, 2, 3):
            for cs in (0, 1):
                send(R.at[(kq + 1) % 4, r, slot(3, cs), 0:128], R.at[kq, r, slot(2, cs), 0:128],
                     rel_s.at[r, 0, cs, kq], rel_r.at[r, 0, cs, kq], dev(dx=1))
                send(R.at[kq - 1, r, slot(1, cs), 128:256], R.at[kq, r, slot(2, cs), 128:256],
                     rel_s.at[r, 1, cs, kq], rel_r.at[r, 1, cs, kq], dev(dx=3))

    def wait_neighbours(r):
        for kq in (1, 2, 3):
            for cs in (0, 1):
                wait_from(r, 1, cs, kq)
                wait_from(r, 3, cs, kq)

    def wait_rest(r):
        for kq in (1, 2, 3):
            wait_from(r, 0, oc, kq)
            for cs in (0, 1):
                for h in (0, 1):
                    arrived(R.at[kq, r, slot(2, cs), h * 128 : h * 128 + 128],
                            rel_r.at[r, h, cs, kq], rel_s.at[0, 0, 0, 1])

    for r in (0, 1):
        wait_from(r, 0, oc, 0)
        for dx in (1, 2, 3):
            for cs in (0, 1):
                wait_from(r, dx, cs, 0)
        send(R.at[0, r], LO.at[r], lo_s.at[r], lo_r.at[r], dev(core=oc))
    arrived(W.at[oc], m_r.at[0, oc], m_s.at[0])
    for dx in (1, 2, 3):
        for cs in (0, 1):
            arrived(W.at[dx * 2 + cs], m_r.at[dx, cs], m_s.at[0])

    def left(src, r, parity):
        block = 2 * x + parity
        base = parity * 512 + r * 256

        def step(k, squares):
            rows = pl.ds(pl.multiple_of(k * 128, 128), 128)
            raw = src[rows, :]
            weight = W[k, pl.ds(block, 1), :]
            for h in (0, 1):
                part = raw[:, h * 128 : h * 128 + 128] * weight
                turned = part.T
                high = turned.astype(BF16)
                low = (turned - high.astype(F32)).astype(BF16)
                at = pl.ds(pl.multiple_of(base + h * 128, 128), 128)
                LTh[at, rows] = high
                LTl[at, rows] = low
            return squares + jnp.sum(raw * raw, axis=0, keepdims=True)

        squares = lax.fori_loop(0, 8, step, jnp.zeros((1, 256), F32))
        for h in (0, 1):
            RSQ[parity * 4 + r * 2 + h] = squares[:, h * 128 : h * 128 + 128]

    for r in (0, 1):
        left(R.at[0, r], r, c)
    for r in (0, 1):
        arrived(LO.at[r], lo_r.at[r], lo_s.at[0])
        left(LO.at[r], r, oc)

    lane_row = lax.broadcasted_iota(jnp.int32, (8, 128), 0)

    def product(r, k, kq):
        src = R.at[kq, r]
        block = 2 * ((x + kq) % 4) + c

        def split(i, squares):
            rows = pl.ds(pl.multiple_of(i * 128, 128), 128)
            raw = src[rows, :]
            weight = W[i, pl.ds(block, 1), :]
            part = raw * jnp.concatenate([weight, weight], axis=1)
            high = part.astype(BF16)
            RH[rows, :] = high
            RL[rows, :] = (part - high.astype(F32)).astype(BF16)
            return squares + jnp.sum(raw * raw, axis=0, keepdims=True)

        squares = lax.fori_loop(0, 8, split, jnp.zeros((1, 256), F32))

        def rows_of(m, carry):
            at = pl.ds(pl.multiple_of(m * 256, 256), 256)
            lh = LTh[at, :]
            ll = LTl[at, :]
            rh = RH[...]
            acc = jnp.dot(lh, rh, preferred_element_type=F32)
            acc += jnp.dot(ll, rh, preferred_element_type=F32)
            acc += jnp.dot(lh, RL[...], preferred_element_type=F32)
            for i in (0, 1):
                for s in (0, 1):
                    D[r, s, k, 2 * m + i, 0:128, :] = acc[i * 128 : i * 128 + 128, s * 128 : s * 128 + 128]
                    extra = jnp.where(lane_row == 0, squares[:, s * 128 : s * 128 + 128], 0.0)
                    D[r, s, k, 2 * m + i, 128:ROWS, :] = jnp.where(lane_row == 1, RSQ[2 * m + i], extra)
            return carry

        lax.fori_loop(0, 4, rows_of, 0)

    def z_chain(chunk, buf, rs, ss, turn):
        def go(zd, j, way):
            send(chunk((z + zd * turn + 8) % 8), buf.at[j], ss.at[j], rs.at[j], dev(dz=way * turn))

        def take(j, zd):
            arrived(buf.at[j], rs.at[j], ss.at[0])
            ref = chunk((z + zd * turn + 8) % 8)
            ref[...] += buf[j]

        def start():
            go(4, 0, 1)
            go(-3, 4, -1)

        def step1():
            take(0, 3)
            go(3, 1, 1)
            take(4, -2)
            go(-2, 5, -1)

        def step2():
            take(1, 2)
            go(2, 2, 1)
            take(5, -1)
            go(-1, 6, -1)

        def step3():
            take(2, 1)
            go(1, 3, 1)
            take(6, 0)

        def finish():
            take(3, 0)

        return start, step1, step2, step3, finish

    def zz(r, k):
        return z_chain(lambda zd: D.at[r, 1, k, zd], ZRz.at[r, k], zz_r.at[r, k], zz_s.at[r, k],
                       1 - 2 * (k % 2))

    def zy(r):
        return z_chain(lambda zd: D.at[r, 0, 3, zd], ZRy.at[r], zy_r.at[r], zy_s.at[r], 1 - 2 * r)

    def y_chain(chunk, buf, rs, ss, turn):
        near, far = (1, 2) if turn == 1 else (2, 1)

        def go(k, j, way):
            send(chunk(k), buf.at[j], ss.at[j], rs.at[j], dev(dy=(way * turn) % 4))

        def take(j, k):
            arrived(buf.at[j], rs.at[j], ss.at[0])
            ref = chunk(k)
            ref[...] += buf[j]

        def start():
            go(0, 0, 1)

        def direct():
            go(far, 2, -1)

        def forward():
            take(0, near)
            go(near, 1, 1)

        def finish():
            take(2, 3)
            take(1, 3)

        return start, direct, forward, finish

    def yy(r, t):
        return y_chain(lambda k: D.at[r, 0, k, t * 4 : t * 4 + 4], YR.at[r, t], yr_r.at[r, t],
                       yr_s.at[r, t], 1 - 2 * t)

    def yz(r):
        return y_chain(lambda k: D.at[r, 1, k, z], YRz.at[r], yz_r.at[r], yz_s.at[r], 1 - 2 * r)

    mine = (x - y + 4) % 4
    k_mine = jnp.where(mine == 2, 0, jnp.where(mine == 1, 1, jnp.where(mine == 3, 2, 3)))

    def rest(r, k):
        kq = (y + OFFS[k] - x + 4) % 4

        @pl.when(kq != 0)
        def _():
            product(r, k, kq)

    yy_chains = {(r, t): yy(r, t) for r in (0, 1) for t in (0, 1)}
    yz_chains = {r: yz(r) for r in (0, 1)}
    zz_chains = {(r, k): zz(r, k) for r in (0, 1) for k in range(4)}
    zy_chains = {r: zy(r) for r in (0, 1)}

    for r in (0, 1):
        product(r, k_mine, 0)

    wait_neighbours(0)
    relay(0)
    for kq in (2, 3):
        own_send(1, kq)
    for kq in (1, 2, 3):
        sibling_send(1, kq)
    wait_rest(0)

    def compute(r):
        rest(r, 0)
        zz_chains[r, 0][0]()
        for t in (0, 1):
            yy_chains[r, t][0]()
        rest(r, 1)
        zz_chains[r, 1][0]()
        yy_chains[r, 1][1]()
        rest(r, 2)
        zz_chains[r, 2][0]()
        yy_chains[r, 0][1]()
        rest(r, 3)
        zz_chains[r, 3][0]()

    def z_round(r, j):
        for k in range(4):
            zz_chains[r, k][j]()

    def middle(r):
        z_round(r, 1)
        for t in (0, 1):
            yy_chains[r, t][2]()
        z_round(r, 2)

    def end(r):
        z_round(r, 3)
        for t in (0, 1):
            yy_chains[r, t][3]()
        zy_chains[r][0]()
        z_round(r, 4)
        yz_chains[r][0]()
        yz_chains[r][1]()
        zy_chains[r][1]()
        yz_chains[r][2]()
        zy_chains[r][2]()
        zy_chains[r][3]()
        yz_chains[r][3]()
        zy_chains[r][4]()

    compute(0)
    middle(0)
    wait_neighbours(1)
    relay(1)
    end(0)
    wait_rest(1)
    compute(1)
    middle(1)
    end(1)

    row_rate = rate_ref[2 * x + z // 4]
    col_rate = rate_ref[2 * y + c]
    row_scale = row_rate * jnp.sqrt(D[0, 0, 3, z, 129:130, :] + EPS)
    row_scale = jnp.broadcast_to(row_scale, (128, 128)).T
    for r in (0, 1):
        for s in (0, 1):
            col_scale = col_rate * jnp.sqrt(D[r, s, 3, z, 128:129, :] + EPS)
            at = r * 256 + s * 128
            CF[:, at : at + 128] = D[r, s, 3, z, 0:128, :] / (row_scale * col_scale)
    half = pl.ds(pl.multiple_of(oc * 64, 64), 64)
    send(CF.at[half, :], out_ref.at[c], f_s, f_r, dev(core=oc))
    out_ref[c] = CF[pl.ds(pl.multiple_of(c * 64, 64), 64), :]
    arrived(out_ref.at[oc], f_r, f_s)
    for copy in pending:
        copy.wait_send()


def per_device(samples, keep_mask, keep_rate):
    weights = jnp.broadcast_to(keep_mask.astype(F32).reshape(8, 1), (8, 128))
    dma = pltpu.SemaphoreType.DMA
    vmem = pltpu.VMEM
    return pl.pallas_call(
        kernel,
        out_shape=jax.ShapeDtypeStruct((2, 64, 512), F32),
        in_specs=[
            pl.BlockSpec(memory_space=pltpu.VMEM),
            pl.BlockSpec(memory_space=pltpu.VMEM),
            pl.BlockSpec(memory_space=pltpu.SMEM),
        ],
        out_specs=pl.BlockSpec(memory_space=pltpu.VMEM),
        scratch_shapes=[
            vmem((4, 2, 1024, 256), F32),
            vmem((2, 1024, 256), F32),
            vmem((8, 8, 128), F32),
            vmem((1024, 1024), BF16),
            vmem((1024, 1024), BF16),
            vmem((1024, 256), BF16),
            vmem((1024, 256), BF16),
            vmem((2, 2, 4, 8, ROWS, 128), F32),
            vmem((8, 1, 128), F32),
            vmem((2, 2, 3, 4, ROWS, 128), F32),
            vmem((2, 3, ROWS, 128), F32),
            vmem((2, 7, ROWS, 128), F32),
            vmem((2, 4, 7, ROWS, 128), F32),
            vmem((128, 512), F32),
            dma((2, 4, 2, 4)),
            dma((2, 2, 2, 4)),
            dma((2, 2, 2, 4)),
            dma((2, 2, 2, 4)),
            dma((2, 2)),
            dma((2, 4)),
            dma((2,)),
            dma((2,)),
            dma((4, 2)),
            dma((8,)),
            dma((2, 2, 3)),
            dma((2, 2, 3)),
            dma((2, 3)),
            dma((2, 3)),
            dma((2, 7)),
            dma((2, 7)),
            dma((2, 4, 7)),
            dma((2, 4, 7)),
            dma,
            dma,
        ],
        compiler_params=pltpu.CompilerParams(
            collective_id=0, has_side_effects=True, vmem_limit_bytes=60 << 20
        ),
        name="sampled_gram",
    )(samples, weights, keep_rate)


def solution(mesh):
    finer = Mesh(mesh.devices.reshape(4, 2, 4, 4, 2), AXES)
    rows = P(AXES, None)
    return jax.shard_map(
        per_device,
        mesh=finer,
        in_specs=(rows, rows, P()),
        out_specs=P(("x", "zh", "y"), ("zl", "c"), None),
        check_vma=False,
    )
```

time: 419 us -> 156 us (0.37)
  waiting for transfers between devices: 290 us -> 0 us
  Pallas kernels: 0 us -> 150 us
  blocking collectives: 69.7 us -> 0 us
  matrix products: 30.1 us -> 0 us
  between operations: 13.2 us -> 0.01 us
  local copies, waits for them, and re-layouts: 6.96 us -> 2.33 us
    all_gather x1 -> x0, waiting for transfers between devices: 175 us -> none  [per_device(): piece = lax.all_gather(masked_rows, ROWS, axis=0, tiled=True)]
    pallas_call x0 -> x1, Pallas kernels: none -> 150 us  [per_device(): pl.pallas_call(kernel, out_shape=jax.ShapeDtypeStruct((2, 64, 512), F32),...]
    reduce_scatter x3 -> x0, waiting for transfers between devices: 115 us -> none  [reduced_to_own(): tiles = lax.psum_scatter(tiles, axes[k], scatter_dimension=0, tiled=True)]
    psum x5 -> x0, blocking collectives: 69.7 us -> none  [one_axis_at_a_time(): value = lax.psum(value, axis)]
    dot_general x1 -> x0, matrix products: 30.1 us -> none  [per_device(): jnp.einsum('rai,rbj->abij', left_cols, right_cols, precision=lax.Precisio...]
    transpose x1 -> x0, local copies, waits for them, and re-layouts: 4.29 us -> none  [reduced_to_own(): tiles = jnp.moveaxis(tiles, turns, range(len(axes))).reshape(-1, *inside)]
  transfers between devices with their start and end apart: 4 -> 0, of which waited for: 3 -> 0; matrix products, arithmetic and copies ran while one was open for 0% -> 0% of each run, Pallas kernels for 0% -> 0%
where the time goes in v1:
time: 156 us; the launch traced here: 153 us
  Pallas kernels  150 us (96%)
  local copies, waits for them, and re-layouts  2.33 us (1%)
    pallas_call x1, Pallas kernels, per_device(): pl.pallas_call(kernel, out_shape=jax.ShapeDtypeStruct((2, 64, 512), F32),...  150 us

profile of v1, /device:TPU:25, one launch (start us, length us, event | category | flops | bytes accessed | tf_op | source)
XLA Modules:
  0.0 153.4 jit_solution(17562133944270120687)
XLA Ops:
  0.0 0.7 convert_bitcast_fusion
  0.7 0.7 broadcast_in_dim.8.w_ref
  1.3 150.4 %sampled_gram.1 = f32[2,64,512]{2,1,0:T(8,128)} custom-call(f32[128,4096]{1,0:T(8,128)} %a_ref.1, f32[8,128]{1,0:T(8,128)} %broadcast_in_dim.8.w_ref, f32[8]{0:T(128)} %rate_ref.1), custom_call_target="tpu_custom_call" | custom-call | tf_op jit(solution)/shard_map/sampled_gram/pallas_call | solution.py:364
  151.7 1.7 %copy.5 = f32[2,64,512]{2,1,0:T(8,128)} copy(f32[2,64,512]{2,1,0:T(8,128)} %sampled_gram.1) | data formatting | bytes 524288

commit v2 on v0

v2 whole, which is shorter than its diff:
```python
import jax
import jax.numpy as jnp
from jax import lax
from jax.experimental import pallas as pl
from jax.experimental.pallas import tpu as pltpu
from jax.sharding import Mesh
from jax.sharding import PartitionSpec as P

AXES = ("x", "zh", "y", "zl", "c")
EPS = 1e-06
MESH = pl.DeviceIdType.MESH
OFFS = (2, 1, 3, 0)
PLACE = {0: 0, 1: 1, 3: 2, 2: 3}
GROUPS = (((1, 1), (1, 2), (1, 3)), ((0, 1), (0, 2), (0, 3)), ((2, 1), (2, 2), (2, 3)), ((3, 1), (3, 2), (3, 3)))
AHEAD = 2
SCHEDULE = (
    ("mul", (0, 0), (3, 0)), ("z", 3, 0, 0), ("z", 0, 0, 0), ("mul", (1, 0), (2, 0)), ("pass", 0),
    ("z", 3, 0, 1), ("z", 0, 0, 1), ("z", 3, 0, 2), ("mul", (1, 1), (1, 2)), ("z", 0, 0, 2), ("mul", (1, 3)),
    ("pass", 1), ("y", 1, 1, 1), ("y", 1, 1, 0), ("y", 1, 0, 1), ("y", 1, 0, 0), ("z", 3, 0, 3),
    ("z", 0, 0, 3), ("z", 3, 0, 4), ("z", 0, 0, 4), ("mul", (0, 1), (0, 2)), ("y", 1, 1, 2), ("z", 0, 2, 0),
    ("z", 0, 1, 0), ("mul", (0, 3)), ("pass", 2), ("z", 0, 3, 0), ("z", 0, 2, 1), ("y", 1, 0, 2),
    ("z", 0, 1, 1), ("z", 0, 3, 1), ("z", 0, 2, 2), ("mul", (2, 1), (2, 2)), ("y", 1, 1, 3), ("pass", 3),
    ("z", 0, 1, 2), ("mul", (2, 3)), ("y", 2, 0, 0), ("y", 2, 1, 0), ("y", 1, 0, 3), ("zy", 1, 0),
    ("y", 2, 1, 1), ("y", 2, 0, 1), ("z", 0, 3, 2), ("z", 0, 2, 3), ("z", 0, 1, 3), ("mul", (3, 1), (3, 2)),
    ("zy", 1, 1), ("z", 3, 1, 0), ("z", 3, 2, 0), ("mul", (3, 3)), ("z", 3, 3, 0), ("z", 0, 3, 3),
    ("z", 0, 2, 4), ("z", 0, 1, 4), ("y", 2, 0, 2), ("y", 2, 1, 2), ("zy", 1, 2), ("z", 3, 1, 1),
    ("z", 3, 2, 1), ("z", 3, 3, 1), ("z", 0, 3, 4), ("yz", 0, 0), ("yz", 0, 1), ("zy", 1, 3), ("z", 3, 1, 2),
    ("y", 2, 1, 3), ("y", 2, 0, 3), ("zy", 2, 0), ("z", 3, 2, 2), ("yz", 0, 2), ("z", 3, 3, 2), ("zy", 1, 4),
    ("z", 3, 1, 3), ("zy", 2, 1), ("yz", 0, 3), ("z", 3, 2, 3), ("z", 3, 3, 3), ("z", 3, 1, 4),
    ("z", 3, 2, 4), ("zy", 2, 2), ("z", 3, 3, 4), ("yz", 3, 0), ("yz", 3, 1), ("zy", 2, 3), ("yz", 3, 2),
    ("zy", 2, 4), ("yz", 3, 3),
)
ROWS = 136
F32 = jnp.float32
BF16 = jnp.bfloat16


def kernel(
    a_ref, mask_ref, rate_ref, out_ref,
    R, LO, W, LTh, LTl, RH, RL, D, RSQ, YR, YRz, ZRy, ZRz, CF,
    ag_r, rel_r, lo_r, m_r, yr_r, yz_r, zy_r, zz_r, f_r,
    own_s, rel_s, sib_s, lo_s, m_s, yr_s, yz_s, zy_s, zz_s, f_s,
):
    x, zh, y, zl, c = (lax.axis_index(a) for a in AXES)
    z = zh * 4 + zl
    oc = 1 - c

    def dev(dx=0, dy=0, dz=0, core=None):
        zz = (z + dz + 8) % 8
        return ((x + dx) % 4, zz // 4, (y + dy) % 4, zz % 4, c if core is None else core)

    def remote(src, dst, ss, rs, to):
        return pltpu.make_async_remote_copy(
            src_ref=src, dst_ref=dst, send_sem=ss, recv_sem=rs, device_id=to, device_id_type=MESH
        )

    def send(src, dst, ss, rs, to):
        remote(src, dst, ss, rs, to).start()

    def arrived(dst, rs):
        remote(dst, dst, f_s, rs, dev(core=oc)).wait_recv()

    def all_sent(ref, ss):
        remote(ref, ref, ss, f_r, dev(core=oc)).wait_send()

    def slot(dx, cs):
        return PLACE[dx] * 2 + cs

    lane_row = lax.broadcasted_iota(jnp.int32, (8, 128), 0)
    weights = jnp.zeros((8, 128), F32)
    for b in range(8):
        weights = jnp.where(lane_row == b, mask_ref[0, b].astype(F32), weights)
    W[slot(0, c)] = weights
    w_ref = W.at[slot(0, c)]

    partners = [dev(dx=d, core=k) for d in (1, 2, 3) for k in (0, 1)] + [dev(core=oc)]
    partners += [dev(dy=1), dev(dy=3), dev(dz=1), dev(dz=7)]
    bar = pltpu.get_barrier_semaphore()
    for p in partners:
        pl.semaphore_signal(bar, inc=1, device_id=p, device_id_type=MESH)
    pl.semaphore_wait(bar, len(partners))

    def cols(q, parity, r):
        return pl.ds(pl.multiple_of((2 * q + parity) * 512 + r * 128, 128), 128)

    def rows_at(dx, cs, half=None):
        first = slot(dx, cs) * 128 + (64 if half == 1 else 0)
        return pl.ds(pl.multiple_of(first, 64), 128 if half is None else 64)

    def half_rows(half):
        return pl.ds(64 if half == 1 else 0, 128 if half is None else 64)

    def own_part(r, kq, d, half):
        for k in (0, 1):
            q = (x + d + kq) % 4
            send(a_ref.at[half_rows(half), cols(q, k, r)], R.at[kq, r, rows_at(4 - d, c, half), :],
                 own_s.at[d // 2], ag_r.at[r, 4 - d, c, kq, half or 0], dev(dx=d, core=k))

    def own_send(r, kq):
        own_part(r, kq, 1, 1 if kq == 1 else None)
        own_part(r, kq, 3, 0 if kq == 3 else None)
        sibling_send(r, kq)

    def sibling_send(r, kq):
        send(a_ref.at[:, cols((x + kq) % 4, oc, r)], R.at[kq, r, rows_at(0, c), :],
             sib_s, ag_r.at[r, 0, c, kq, 0], dev(core=oc))

    def wait_part(r, dx, cs, kq, half):
        arrived(R.at[kq, r, rows_at(dx, cs, half), :], ag_r.at[r, dx, cs, kq, half or 0])

    def relay(r, kq):
        for cs in (0, 1):
            send(R.at[(kq + 1) % 4, r, rows_at(3, cs, 0), :], R.at[kq, r, rows_at(2, cs, 0), :],
                 rel_s.at[0], rel_r.at[r, 0, cs, kq], dev(dx=1))
            send(R.at[(kq + 3) % 4, r, rows_at(1, cs, 1), :], R.at[kq, r, rows_at(2, cs, 1), :],
                 rel_s.at[1], rel_r.at[r, 1, cs, kq], dev(dx=3))

    def wait_relayed(r, kq):
        for cs in (0, 1):
            for h in (0, 1):
                arrived(R.at[kq, r, rows_at(2, cs, h), :], rel_r.at[r, h, cs, kq])

    def wait_neighbours(r, kq):
        for cs in (0, 1):
            wait_part(r, 3, cs, kq, 1 if kq == 1 else None)
            wait_part(r, 1, cs, kq, 0 if kq == 3 else None)

    def wait_rest(r, kq):
        wait_part(r, 0, oc, kq, None)
        wait_relayed(r, kq)

    units = [u for group in GROUPS for u in group]
    sent = [0]

    def own_sends(upto):
        for u in units[sent[0] : upto]:
            own_send(*u)
        sent[0] = max(sent[0], upto)

    def pass_on(i):
        for u in GROUPS[i]:
            wait_neighbours(*u)
        for u in GROUPS[i]:
            relay(*u)
        own_sends(sum(len(group) for group in GROUPS[: i + 2]) + AHEAD)

    for d in (1, 2, 3):
        for k in (0, 1):
            send(w_ref, W.at[slot(4 - d, c)], m_s.at[d * 2 + k], m_r.at[4 - d, c], dev(dx=d, core=k))
    send(w_ref, W.at[slot(0, c)], m_s.at[0], m_r.at[0, c], dev(core=oc))
    for r in range(4):
        own_part(r, 1, 1, 0)
        own_part(r, 3, 3, 1)
    for r in range(4):
        own_part(r, 0, 1, None)
        own_part(r, 0, 3, None)
        sibling_send(r, 0)

    for r in range(4):
        for kq in range(4):
            R[kq, r, rows_at(0, c), :] = a_ref[:, cols((x + kq) % 4, c, r)]

    for r in range(4):
        for cs in (0, 1):
            wait_part(r, 3, cs, 1, 0)
            wait_part(r, 1, cs, 3, 1)
        relay(r, 0)
    own_sends(len(GROUPS[0]) + AHEAD)

    def left(src, r, parity, first, last):
        block = 2 * x + parity
        at = pl.ds(pl.multiple_of(parity * 512 + r * 128, 128), 128)

        def step(k, squares):
            rows = pl.ds(pl.multiple_of(k * 128, 128), 128)
            raw = src[rows, :]
            turned = (raw * W[k, pl.ds(block, 1), :]).T
            high = turned.astype(BF16)
            LTh[at, rows] = high
            LTl[at, rows] = (turned - high.astype(F32)).astype(BF16)
            return squares + jnp.sum(raw * raw, axis=0, keepdims=True)

        before = RSQ[parity * 4 + r] if first else jnp.zeros((1, 128), F32)
        RSQ[parity * 4 + r] = lax.fori_loop(first, last, step, before)

    for r in range(4):
        wait_part(r, 0, oc, 0, None)
        for cs in (0, 1):
            wait_part(r, 1, cs, 0, None)
            wait_part(r, 3, cs, 0, None)
        send(R.at[0, r, 0:768], LO.at[r, 0:768], lo_s, lo_r.at[r, 0], dev(core=oc))
    arrived(W.at[slot(0, oc)], m_r.at[0, oc])
    for dx in (1, 2, 3):
        for cs in (0, 1):
            arrived(W.at[slot(dx, cs)], m_r.at[dx, cs])
    for r in range(4):
        left(R.at[0, r], r, c, 0, 6)
        arrived(LO.at[r, 0:768], lo_r.at[r, 0])
        left(LO.at[r], r, oc, 0, 6)
    for r in range(4):
        wait_relayed(r, 0)
        send(R.at[0, r, 768:1024], LO.at[r, 768:1024], lo_s, lo_r.at[r, 1], dev(core=oc))
        left(R.at[0, r], r, c, 6, 8)
    for r in range(4):
        arrived(LO.at[r, 768:1024], lo_r.at[r, 1])
        left(LO.at[r], r, oc, 6, 8)

    def product(*units):
        width = 128 * len(units)
        squares = []
        for j, (r, kq) in enumerate(units):
            src = R.at[kq, r]
            block = 2 * ((x + kq) % 4) + c
            at = slice(j * 128, j * 128 + 128)

            def split(i, total):
                rows = pl.ds(pl.multiple_of(i * 128, 128), 128)
                raw = src[rows, :]
                part = raw * W[i, pl.ds(block, 1), :]
                high = part.astype(BF16)
                RH[rows, at] = high
                RL[rows, at] = (part - high.astype(F32)).astype(BF16)
                return total + jnp.sum(raw * raw, axis=0, keepdims=True)

            squares.append(lax.fori_loop(0, 8, split, jnp.zeros((1, 128), F32)))

        def rows_of(m, carry):
            at = pl.ds(pl.multiple_of(m * 512, 512), 512)
            lh = LTh[at, :]
            rh = RH[:, 0:width]
            acc = jnp.dot(lh, rh, preferred_element_type=F32)
            acc += jnp.dot(LTl[at, :], rh, preferred_element_type=F32)
            acc += jnp.dot(lh, RL[:, 0:width], preferred_element_type=F32)
            for i in range(4):
                zd = 4 * m + i
                for j, (r, kq) in enumerate(units):
                    D[r, kq, zd, 0:128, :] = acc[i * 128 : i * 128 + 128, j * 128 : j * 128 + 128]
                    extra = jnp.where(lane_row == 0, squares[j], 0.0)
                    D[r, kq, zd, 128:ROWS, :] = jnp.where(lane_row == 1, RSQ[zd], extra)
            return carry

        lax.fori_loop(0, 2, rows_of, 0)

    def z_chain(chunk, buf, rs, ss, turn):
        def go(zd, j, way):
            send(chunk((z + zd * turn + 8) % 8), buf.at[j], ss, rs.at[j], dev(dz=way * turn))

        def take(j, zd):
            arrived(buf.at[j], rs.at[j])
            ref = chunk((z + zd * turn + 8) % 8)
            ref[...] += buf[j]

        def start():
            go(4, 0, 1)
            go(-3, 4, -1)

        def step1():
            take(0, 3)
            go(3, 1, 1)
            take(4, -2)
            go(-2, 5, -1)

        def step2():
            take(1, 2)
            go(2, 2, 1)
            take(5, -1)
            go(-1, 6, -1)

        def step3():
            take(2, 1)
            go(1, 3, 1)
            take(6, 0)

        def finish():
            take(3, 0)

        return start, step1, step2, step3, finish

    def y_chain(chunk, buf, rs, ss, turn):
        near, far = (1, 2) if turn == 1 else (2, 1)

        def go(k, j, way):
            send(chunk(k), buf.at[j], ss, rs.at[j], dev(dy=(way * turn) % 4))

        def take(j, k):
            arrived(buf.at[j], rs.at[j])
            ref = chunk(k)
            ref[...] += buf[j]

        def start():
            go(0, 0, 1)

        def direct():
            go(far, 2, -1)

        def forward():
            take(0, near)
            go(near, 1, 1)

        def finish():
            take(2, 3)
            take(1, 3)

        return start, direct, forward, finish

    kqs = [(y + off - x + 4) % 4 for off in OFFS]

    def zz(r, kq):
        i = r // 3
        return z_chain(lambda zd: D.at[r, kq, zd], ZRz.at[i, kq], zz_r.at[i, kq], zz_s.at[i, kq],
                       1 - 2 * ((kq + i) % 2))

    def zy(r):
        i = r - 1
        return z_chain(lambda zd: D.at[r, kqs[3], zd], ZRy.at[i], zy_r.at[i], zy_s.at[i], 1 - 2 * i)

    def yy(r, t):
        i = r - 1
        return y_chain(lambda k: D.at[r, kqs[k], t * 4 : t * 4 + 4], YR.at[i, t], yr_r.at[i, t],
                       yr_s.at[i, t], 1 - 2 * t)

    def yz(r):
        i = r // 3
        return y_chain(lambda k: D.at[r, kqs[k], z], YRz.at[i], yz_r.at[i], yz_s.at[i], 1 - 2 * i)

    ZZ = {(r, kq): zz(r, kq) for r in (0, 3) for kq in range(4)}
    ZY = {r: zy(r) for r in (1, 2)}
    YY = {(r, t): yy(r, t) for r in (1, 2) for t in (0, 1)}
    YZ = {r: yz(r) for r in (0, 3)}

    def y_begin(r, early):
        for k in range(3):

            @pl.when((kqs[k] == 0) == early)
            def _():
                if k == 0:
                    YY[r, 0][0]()
                    YY[r, 1][0]()
                else:
                    YY[r, 2 - k][1]()

    begun = set()
    for name, *key in SCHEDULE:
        if name == "mul":
            for u in key:
                if u[1]:
                    wait_rest(*u)
            product(*key)
            for r, kq in key:
                if kq == 0 and r in (1, 2):
                    y_begin(r, True)
        elif name == "pass":
            pass_on(*key)
        elif name == "z":
            ZZ[key[0], key[1]][key[2]]()
        elif name == "zy":
            ZY[key[0]][key[1]]()
        elif name == "yz":
            YZ[key[0]][key[1]]()
        elif key[2] > 1:
            YY[key[0], key[1]][key[2]]()
        elif key[0] not in begun:
            begun.add(key[0])
            y_begin(key[0], False)

    own = kqs[3]
    row_rate = rate_ref[2 * x + z // 4]
    col_rate = rate_ref[2 * y + c]
    row_scale = row_rate * jnp.sqrt(D[0, own, z, 129:130, :] + EPS)
    row_scale = jnp.broadcast_to(row_scale, (128, 128)).T
    for r in range(4):
        col_scale = col_rate * jnp.sqrt(D[r, own, z, 128:129, :] + EPS)
        CF[:, r * 128 : r * 128 + 128] = D[r, own, z, 0:128, :] / (row_scale * col_scale)
    half = pl.ds(pl.multiple_of(oc * 64, 64), 64)
    send(CF.at[half, :], out_ref.at[c], f_s, f_r, dev(core=oc))
    out_ref[c] = CF[pl.ds(pl.multiple_of(c * 64, 64), 64), :]
    arrived(out_ref.at[oc], f_r)
    all_sent(CF.at[half, :], f_s)
    for i in range(2):
        all_sent(a_ref, own_s.at[i])
        all_sent(a_ref.at[:, 0:2048], rel_s.at[i])
        all_sent(YRz.at[i], yz_s.at[i])
        all_sent(ZRy.at[i], zy_s.at[i])
        for t in range(2):
            all_sent(YR.at[i, t], yr_s.at[i, t])
        for kq in range(4):
            all_sent(ZRz.at[i, kq], zz_s.at[i, kq])
    all_sent(a_ref.at[:, 0:2048], sib_s)
    all_sent(LO, lo_s)
    for i in [0] + list(range(2, 8)):
        all_sent(w_ref, m_s.at[i])


def per_device(samples, keep_mask, keep_rate):
    dma = pltpu.SemaphoreType.DMA
    vmem = pltpu.VMEM
    return pl.pallas_call(
        kernel,
        out_shape=jax.ShapeDtypeStruct((2, 64, 512), F32),
        in_specs=[
            pl.BlockSpec(memory_space=pltpu.VMEM),
            pl.BlockSpec(memory_space=pltpu.SMEM),
            pl.BlockSpec(memory_space=pltpu.SMEM),
        ],
        out_specs=pl.BlockSpec(memory_space=pltpu.VMEM),
        scratch_shapes=[
            vmem((4, 4, 1024, 128), F32),
            vmem((4, 1024, 128), F32),
            vmem((8, 8, 128), F32),
            vmem((1024, 1024), BF16),
            vmem((1024, 1024), BF16),
            vmem((1024, 256), BF16),
            vmem((1024, 256), BF16),
            vmem((4, 4, 8, ROWS, 128), F32),
            vmem((8, 1, 128), F32),
            vmem((2, 2, 3, 4, ROWS, 128), F32),
            vmem((2, 3, ROWS, 128), F32),
            vmem((2, 7, ROWS, 128), F32),
            vmem((2, 4, 7, ROWS, 128), F32),
            vmem((128, 512), F32),
            dma((4, 4, 2, 4, 2)),
            dma((4, 2, 2, 4)),
            dma((4, 2)),
            dma((4, 2)),
            dma((2, 2, 3)),
            dma((2, 3)),
            dma((2, 7)),
            dma((2, 4, 7)),
            dma,
            dma((2,)),
            dma((2,)),
            dma,
            dma,
            dma((8,)),
            dma((2, 2)),
            dma((2,)),
            dma((2,)),
            dma((2, 4)),
            dma,
        ],
        compiler_params=pltpu.CompilerParams(
            collective_id=0, has_side_effects=True, vmem_limit_bytes=60 << 20
        ),
        name="sampled_gram",
    )(samples, keep_mask, keep_rate)


def solution(mesh):
    finer = Mesh(mesh.devices.reshape(4, 2, 4, 4, 2), AXES)
    rows = P(AXES, None)
    return jax.shard_map(
        per_device,
        mesh=finer,
        in_specs=(rows, rows, P()),
        out_specs=P(("x", "zh", "y"), ("zl", "c"), None),
        check_vma=False,
    )
```

time: 419 us -> 126 us (0.30)
  waiting for transfers between devices: 290 us -> 0 us
  Pallas kernels: 0 us -> 122 us
  blocking collectives: 69.7 us -> 0 us
  matrix products: 30.1 us -> 0 us
  between operations: 13.2 us -> 0.01 us
  local copies, waits for them, and re-layouts: 6.96 us -> 1.67 us
  other arithmetic: 4.7 us -> 0 us
    all_gather x1 -> x0, waiting for transfers between devices: 175 us -> none  [per_device(): piece = lax.all_gather(masked_rows, ROWS, axis=0, tiled=True)]
    pallas_call x0 -> x1, Pallas kernels: none -> 122 us  [per_device(): pl.pallas_call(kernel, out_shape=jax.ShapeDtypeStruct((2, 64, 512), F32),...]
    reduce_scatter x3 -> x0, waiting for transfers between devices: 115 us -> none  [reduced_to_own(): tiles = lax.psum_scatter(tiles, axes[k], scatter_dimension=0, tiled=True)]
    psum x5 -> x0, blocking collectives: 69.7 us -> none  [one_axis_at_a_time(): value = lax.psum(value, axis)]
    dot_general x1 -> x0, matrix products: 30.1 us -> none  [per_device(): jnp.einsum('rai,rbj->abij', left_cols, right_cols, precision=lax.Precisio...]
    transpose x1 -> x0, local copies, waits for them, and re-layouts: 4.29 us -> none  [reduced_to_own(): tiles = jnp.moveaxis(tiles, turns, range(len(axes))).reshape(-1, *inside)]
  transfers between devices with their start and end apart: 4 -> 0, of which waited for: 3 -> 0; matrix products, arithmetic and copies ran while one was open for 0% -> 0% of each run, Pallas kernels for 0% -> 0%
where the time goes in v2:
time: 126 us; the launch traced here: 124 us
  Pallas kernels  122 us (97%)
  local copies, waits for them, and re-layouts  1.67 us (1%)
    pallas_call x1, Pallas kernels, per_device(): pl.pallas_call(kernel, out_shape=jax.ShapeDtypeStruct((2, 64, 512), F32),...  122 us

profile of v2, /device:TPU:25, one launch (start us, length us, event | category | flops | bytes accessed | tf_op | source)
XLA Modules:
  0.0 124.0 jit_solution(4440707332179126447)
XLA Ops:
  0.0 122.4 %sampled_gram.1 = f32[2,64,512]{2,1,0:T(8,128)} custom-call(f32[128,4096]{1,0:T(8,128)} %a_ref.1, s32[1,8]{1,0:T(1,128)} %mask_ref.1, f32[8]{0:T(128)} %rate_ref.1), custom_call_target="tpu_custom_call" | custom-call | tf_op jit(solution)/shard_map/sampled_gram/pallas_call | solution.py:397
  122.4 1.7 %copy.5 = f32[2,64,512]{2,1,0:T(8,128)} copy(f32[2,64,512]{2,1,0:T(8,128)} %sampled_gram.1) | data formatting | bytes 524288

commit v3 on v2

--- a/solution.py
+++ b/solution.py
@@ -11,24 +11,31 @@
 MESH = pl.DeviceIdType.MESH
 OFFS = (2, 1, 3, 0)
 PLACE = {0: 0, 1: 1, 3: 2, 2: 3}
-GROUPS = (((1, 1), (1, 2), (1, 3)), ((0, 1), (0, 2), (0, 3)), ((2, 1), (2, 2), (2, 3)), ((3, 1), (3, 2), (3, 3)))
-AHEAD = 2
+GROUPS = (((1, 1), (2, 1)), ((0, 1), (3, 1)), ((1, 2), (2, 2)), ((0, 2), (3, 2)))
+AHEAD = 1
 SCHEDULE = (
-    ("mul", (0, 0), (3, 0)), ("z", 3, 0, 0), ("z", 0, 0, 0), ("mul", (1, 0), (2, 0)), ("pass", 0),
-    ("z", 3, 0, 1), ("z", 0, 0, 1), ("z", 3, 0, 2), ("mul", (1, 1), (1, 2)), ("z", 0, 0, 2), ("mul", (1, 3)),
-    ("pass", 1), ("y", 1, 1, 1), ("y", 1, 1, 0), ("y", 1, 0, 1), ("y", 1, 0, 0), ("z", 3, 0, 3),
-    ("z", 0, 0, 3), ("z", 3, 0, 4), ("z", 0, 0, 4), ("mul", (0, 1), (0, 2)), ("y", 1, 1, 2), ("z", 0, 2, 0),
-    ("z", 0, 1, 0), ("mul", (0, 3)), ("pass", 2), ("z", 0, 3, 0), ("z", 0, 2, 1), ("y", 1, 0, 2),
-    ("z", 0, 1, 1), ("z", 0, 3, 1), ("z", 0, 2, 2), ("mul", (2, 1), (2, 2)), ("y", 1, 1, 3), ("pass", 3),
-    ("z", 0, 1, 2), ("mul", (2, 3)), ("y", 2, 0, 0), ("y", 2, 1, 0), ("y", 1, 0, 3), ("zy", 1, 0),
-    ("y", 2, 1, 1), ("y", 2, 0, 1), ("z", 0, 3, 2), ("z", 0, 2, 3), ("z", 0, 1, 3), ("mul", (3, 1), (3, 2)),
-    ("zy", 1, 1), ("z", 3, 1, 0), ("z", 3, 2, 0), ("mul", (3, 3)), ("z", 3, 3, 0), ("z", 0, 3, 3),
-    ("z", 0, 2, 4), ("z", 0, 1, 4), ("y", 2, 0, 2), ("y", 2, 1, 2), ("zy", 1, 2), ("z", 3, 1, 1),
-    ("z", 3, 2, 1), ("z", 3, 3, 1), ("z", 0, 3, 4), ("yz", 0, 0), ("yz", 0, 1), ("zy", 1, 3), ("z", 3, 1, 2),
-    ("y", 2, 1, 3), ("y", 2, 0, 3), ("zy", 2, 0), ("z", 3, 2, 2), ("yz", 0, 2), ("z", 3, 3, 2), ("zy", 1, 4),
-    ("z", 3, 1, 3), ("zy", 2, 1), ("yz", 0, 3), ("z", 3, 2, 3), ("z", 3, 3, 3), ("z", 3, 1, 4),
-    ("z", 3, 2, 4), ("zy", 2, 2), ("z", 3, 3, 4), ("yz", 3, 0), ("yz", 3, 1), ("zy", 2, 3), ("yz", 3, 2),
-    ("zy", 2, 4), ("yz", 3, 3),
+    ("mul", (1, 0), (2, 0)), ("y", 2, 0, 0, 0), ("y", 1, 0, 1, 0), ("y", 1, 0, 0, 0), ("y", 2, 0, 1, 0),
+    ("mul", (0, 0), (3, 0)), ("pass", 0), ("z", 3, 0, 0), ("z", 0, 0, 0), ("z", 3, 0, 1),
+    ("mul", (1, 1), (2, 1)), ("y", 1, 1, 1, 0), ("y", 2, 1, 1, 0), ("y", 1, 1, 0, 0), ("y", 2, 1, 0, 0),
+    ("y", 2, 0, 0, 1), ("z", 0, 0, 1), ("y", 1, 0, 1, 1), ("pass", 1), ("z", 3, 0, 2), ("y", 1, 0, 0, 1),
+    ("z", 0, 0, 2), ("y", 2, 0, 1, 1), ("mul", (0, 1), (3, 1)), ("y", 1, 1, 1, 1), ("z", 3, 1, 0),
+    ("z", 0, 1, 0), ("z", 3, 0, 3), ("pass", 2), ("z", 0, 0, 3), ("y", 2, 1, 1, 1), ("z", 3, 1, 1),
+    ("y", 1, 1, 0, 1), ("y", 2, 1, 0, 1), ("z", 0, 1, 1), ("mul", (1, 2), (2, 2)), ("y", 1, 2, 1, 0),
+    ("y", 1, 0, 1, 2), ("z", 3, 0, 4), ("yz", 3, 0, 0), ("y", 2, 2, 0, 0), ("y", 2, 0, 0, 2), ("pass", 3),
+    ("y", 2, 2, 1, 0), ("z", 3, 1, 2), ("y", 1, 2, 0, 0), ("z", 0, 0, 4), ("yz", 0, 0, 0), ("y", 1, 0, 0, 2),
+    ("y", 2, 0, 1, 2), ("zy", 1, 0, 0), ("zy", 2, 0, 0), ("z", 0, 1, 2), ("y", 1, 1, 1, 2), ("z", 3, 1, 3),
+    ("y", 1, 1, 0, 2), ("zy", 1, 1, 0), ("y", 2, 1, 1, 2), ("yz", 3, 0, 1), ("mul", (0, 2), (3, 2)),
+    ("zy", 1, 0, 1), ("zy", 2, 0, 1), ("y", 1, 2, 1, 1), ("y", 2, 1, 0, 2), ("zy", 2, 1, 0), ("z", 0, 1, 3),
+    ("z", 0, 2, 0), ("z", 3, 2, 0), ("z", 3, 1, 4), ("yz", 3, 1, 0), ("y", 2, 2, 0, 1), ("zy", 1, 1, 1),
+    ("zy", 1, 0, 2), ("yz", 0, 0, 1), ("y", 2, 2, 1, 1), ("yz", 3, 0, 2), ("zy", 2, 0, 2), ("zy", 2, 1, 1),
+    ("z", 0, 1, 4), ("yz", 0, 1, 0), ("y", 1, 2, 0, 1), ("z", 0, 2, 1), ("yz", 3, 1, 1), ("z", 3, 2, 1),
+    ("yz", 0, 0, 2), ("y", 1, 2, 1, 2), ("yz", 0, 1, 1), ("zy", 1, 1, 2), ("zy", 1, 0, 3), ("y", 2, 2, 0, 2),
+    ("yz", 3, 1, 2), ("zy", 2, 0, 3), ("zy", 2, 1, 2), ("z", 0, 2, 2), ("y", 2, 2, 1, 2), ("zy", 2, 2, 0),
+    ("yz", 0, 1, 2), ("y", 1, 2, 0, 2), ("zy", 1, 2, 0), ("z", 3, 2, 2), ("zy", 1, 0, 4), ("zy", 1, 1, 3),
+    ("zy", 2, 0, 4), ("zy", 2, 1, 3), ("z", 0, 2, 3), ("zy", 2, 2, 1), ("zy", 1, 2, 1), ("z", 3, 2, 3),
+    ("zy", 1, 1, 4), ("zy", 2, 1, 4), ("turn",), ("z", 0, 2, 4), ("yz", 0, 2, 0), ("zy", 2, 2, 2),
+    ("zy", 1, 2, 2), ("z", 3, 2, 4), ("yz", 3, 2, 0), ("yz", 0, 2, 1), ("zy", 2, 2, 3), ("zy", 1, 2, 3),
+    ("yz", 3, 2, 1), ("yz", 0, 2, 2), ("yz", 3, 2, 2), ("zy", 2, 2, 4), ("zy", 1, 2, 4),
 )
 ROWS = 136
 F32 = jnp.float32
@@ -36,10 +43,10 @@
 
 
 def kernel(
-    a_ref, mask_ref, rate_ref, out_ref,
-    R, LO, W, LTh, LTl, RH, RL, D, RSQ, YR, YRz, ZRy, ZRz, CF,
-    ag_r, rel_r, lo_r, m_r, yr_r, yz_r, zy_r, zz_r, f_r,
-    own_s, rel_s, sib_s, lo_s, m_s, yr_s, yz_s, zy_s, zz_s, f_s,
+    in_ref, mask_ref, rate_ref, out_ref,
+    a_ref, R, LO, W, LTh, LTl, RH, RL, D, RSQ, YR, YRz, ZRy, ZRz, CF, TB,
+    ag_r, rel_r, lo_r, m_r, yr_r, yz_r, zy_r, zz_r, tb_r, f_r,
+    own_s, rel_s, sib_s, lo_s, m_s, yr_s, yz_s, zy_s, zz_s, tb_s, f_s, in_s,
 ):
     x, zh, y, zl, c = (lax.axis_index(a) for a in AXES)
     z = zh * 4 + zl
@@ -62,6 +69,9 @@
 
     def all_sent(ref, ss):
         remote(ref, ref, ss, f_r, dev(core=oc)).wait_send()
+
+    load = pltpu.make_async_copy(in_ref, a_ref, in_s)
+    load.start()
 
     def slot(dx, cs):
         return PLACE[dx] * 2 + cs
@@ -79,6 +89,10 @@
     for p in partners:
         pl.semaphore_signal(bar, inc=1, device_id=p, device_id_type=MESH)
     pl.semaphore_wait(bar, len(partners))
+    kqs = [(y + off - x + 4) % 4 for off in OFFS]
+    own = kqs[3]
+    takers = [((x + 1) % 4, c, (y + 3) % 4, g, zh) for g in range(4)]
+    load.wait()
 
     def cols(q, parity, r):
         return pl.ds(pl.multiple_of((2 * q + parity) * 512 + r * 128, 128), 128)
@@ -97,8 +111,9 @@
                  own_s.at[d // 2], ag_r.at[r, 4 - d, c, kq, half or 0], dev(dx=d, core=k))
 
     def own_send(r, kq):
-        own_part(r, kq, 1, 1 if kq == 1 else None)
-        own_part(r, kq, 3, 0 if kq == 3 else None)
+        own_part(r, kq, 1, 1)
+        own_part(r, kq + 1, 1, 0)
+        own_part(r, kq, 3, None)
         sibling_send(r, kq)
 
     def sibling_send(r, kq):
@@ -122,8 +137,9 @@
 
     def wait_neighbours(r, kq):
         for cs in (0, 1):
-            wait_part(r, 3, cs, kq, 1 if kq == 1 else None)
-            wait_part(r, 1, cs, kq, 0 if kq == 3 else None)
+            wait_part(r, 3, cs, kq, 1)
+            wait_part(r, 3, cs, kq + 1, 0)
+            wait_part(r, 1, cs, kq, None)
 
     def wait_rest(r, kq):
         wait_part(r, 0, oc, kq, None)
@@ -157,7 +173,7 @@
         sibling_send(r, 0)
 
     for r in range(4):
-        for kq in range(4):
+        for kq in range(3):
             R[kq, r, rows_at(0, c), :] = a_ref[:, cols((x + kq) % 4, c, r)]
 
     for r in range(4):
@@ -276,116 +292,135 @@
 
         return start, step1, step2, step3, finish
 
-    def y_chain(chunk, buf, rs, ss, turn):
+    def y_chain(kq, ref, buf, rs, ss, turn):
         near, far = (1, 2) if turn == 1 else (2, 1)
 
-        def go(k, j, way):
-            send(chunk(k), buf.at[j], ss, rs.at[j], dev(dy=(way * turn) % 4))
-
-        def take(j, k):
+        def go(j, way):
+            send(ref, buf.at[j], ss.at[j], rs.at[j], dev(dy=(way * turn) % 4))
+
+        def take(j):
             arrived(buf.at[j], rs.at[j])
-            ref = chunk(k)
             ref[...] += buf[j]
 
-        def start():
-            go(0, 0, 1)
-
-        def direct():
-            go(far, 2, -1)
+        def begin():
+            @pl.when(kqs[0] == kq)
+            def _():
+                go(0, 1)
+
+            @pl.when(kqs[far] == kq)
+            def _():
+                go(2, -1)
 
         def forward():
-            take(0, near)
-            go(near, 1, 1)
+            @pl.when(kqs[near] == kq)
+            def _():
+                take(0)
+                go(1, 1)
 
         def finish():
-            take(2, 3)
-            take(1, 3)
-
-        return start, direct, forward, finish
-
-    kqs = [(y + off - x + 4) % 4 for off in OFFS]
+            @pl.when(own == kq)
+            def _():
+                take(2)
+                take(1)
+
+        return begin, forward, finish
+
+    def y_sent(buf, ss, turn):
+        for k, j in ((0, 0), (1, 1 if turn == 1 else 2), (2, 2 if turn == 1 else 1)):
+
+            @pl.when(kqs[k] != 3)
+            def _():
+                all_sent(buf.at[j], ss.at[j])
 
     def zz(r, kq):
         i = r // 3
         return z_chain(lambda zd: D.at[r, kq, zd], ZRz.at[i, kq], zz_r.at[i, kq], zz_s.at[i, kq],
                        1 - 2 * ((kq + i) % 2))
 
-    def zy(r):
+    def zy(r, kq):
         i = r - 1
-        return z_chain(lambda zd: D.at[r, kqs[3], zd], ZRy.at[i], zy_r.at[i], zy_s.at[i], 1 - 2 * i)
-
-    def yy(r, t):
+        return z_chain(lambda zd: D.at[r, kq, zd], ZRy.at[i], zy_r.at[i], zy_s.at[i], 1 - 2 * (r % 2 == 0))
+
+    def yy(r, kq, t):
         i = r - 1
-        return y_chain(lambda k: D.at[r, kqs[k], t * 4 : t * 4 + 4], YR.at[i, t], yr_r.at[i, t],
-                       yr_s.at[i, t], 1 - 2 * t)
-
-    def yz(r):
+        return y_chain(kq, D.at[r, kq, t * 4 : t * 4 + 4], YR.at[i, t], yr_r.at[i, t], yr_s.at[i, t],
+                       1 - 2 * t)
+
+    def yz(r, kq):
         i = r // 3
-        return y_chain(lambda k: D.at[r, kqs[k], z], YRz.at[i], yz_r.at[i], yz_s.at[i], 1 - 2 * i)
-
-    ZZ = {(r, kq): zz(r, kq) for r in (0, 3) for kq in range(4)}
-    ZY = {r: zy(r) for r in (1, 2)}
-    YY = {(r, t): yy(r, t) for r in (1, 2) for t in (0, 1)}
-    YZ = {r: yz(r) for r in (0, 3)}
-
-    def y_begin(r, early):
-        for k in range(3):
-
-            @pl.when((kqs[k] == 0) == early)
-            def _():
-                if k == 0:
-                    YY[r, 0][0]()
-                    YY[r, 1][0]()
-                else:
-                    YY[r, 2 - k][1]()
-
-    begun = set()
+        return y_chain(kq, D.at[r, kq, z], YRz.at[i], yz_r.at[i], yz_s.at[i], 1 - 2 * i)
+
+    def cosines():
+        row_rate = rate_ref[2 * x + z // 4]
+        col_rate = rate_ref[2 * y + c]
+        row_scale = row_rate * jnp.sqrt(D[0, own, z, 129:130, :] + EPS)
+        row_scale = jnp.broadcast_to(row_scale, (128, 128)).T
+        for r in range(4):
+            col_scale = col_rate * jnp.sqrt(D[r, own, z, 128:129, :] + EPS)
+            CF[:, r * 128 : r * 128 + 128] = D[r, own, z, 0:128, :] / (row_scale * col_scale)
+
     for name, *key in SCHEDULE:
         if name == "mul":
             for u in key:
                 if u[1]:
                     wait_rest(*u)
             product(*key)
-            for r, kq in key:
-                if kq == 0 and r in (1, 2):
-                    y_begin(r, True)
         elif name == "pass":
             pass_on(*key)
         elif name == "z":
-            ZZ[key[0], key[1]][key[2]]()
+            zz(*key[:2])[key[2]]()
+        elif name == "yz":
+            yz(*key[:2])[key[2]]()
+        elif name == "y":
+            yy(*key[:3])[key[3]]()
         elif name == "zy":
-            ZY[key[0]][key[1]]()
-        elif name == "yz":
-            YZ[key[0]][key[1]]()
-        elif key[2] > 1:
-            YY[key[0], key[1]][key[2]]()
-        elif key[0] not in begun:
-            begun.add(key[0])
-            y_begin(key[0], False)
-
-    own = kqs[3]
-    row_rate = rate_ref[2 * x + z // 4]
-    col_rate = rate_ref[2 * y + c]
-    row_scale = row_rate * jnp.sqrt(D[0, own, z, 129:130, :] + EPS)
-    row_scale = jnp.broadcast_to(row_scale, (128, 128)).T
-    for r in range(4):
-        col_scale = col_rate * jnp.sqrt(D[r, own, z, 128:129, :] + EPS)
-        CF[:, r * 128 : r * 128 + 128] = D[r, own, z, 0:128, :] / (row_scale * col_scale)
+
+            @pl.when(own == key[1])
+            def _():
+                zy(*key[:2])[key[2]]()
+
+        else:
+
+            @pl.when(own == 1)
+            def _():
+                cosines()
+                for g in range(4):
+                    send(CF.at[:, g * 128 : g * 128 + 128], TB.at[zl], tb_s.at[g], tb_r.at[zl], takers[g])
+
+    @pl.when((own == 0) | (own == 2))
+    def _():
+        cosines()
+
+    @pl.when(own == 3)
+    def _():
+        for g in range(4):
+            arrived(TB.at[g], tb_r.at[g])
+            CF[:, g * 128 : g * 128 + 128] = TB[g].T
+
     half = pl.ds(pl.multiple_of(oc * 64, 64), 64)
     send(CF.at[half, :], out_ref.at[c], f_s, f_r, dev(core=oc))
     out_ref[c] = CF[pl.ds(pl.multiple_of(c * 64, 64), 64), :]
     arrived(out_ref.at[oc], f_r)
     all_sent(CF.at[half, :], f_s)
     for i in range(2):
-        all_sent(a_ref, own_s.at[i])
-        all_sent(a_ref.at[:, 0:2048], rel_s.at[i])
-        all_sent(YRz.at[i], yz_s.at[i])
-        all_sent(ZRy.at[i], zy_s.at[i])
+        all_sent(a_ref.at[:, 0:3584], own_s.at[i])
+        all_sent(a_ref.at[:, 0:1536], rel_s.at[i])
+        y_sent(YRz.at[i], yz_s.at[i], 1 - 2 * i)
         for t in range(2):
-            all_sent(YR.at[i, t], yr_s.at[i, t])
-        for kq in range(4):
+            y_sent(YR.at[i, t], yr_s.at[i, t], 1 - 2 * t)
+        for kq in range(3):
             all_sent(ZRz.at[i, kq], zz_s.at[i, kq])
-    all_sent(a_ref.at[:, 0:2048], sib_s)
+
+        @pl.when(own != 3)
+        def _():
+            all_sent(ZRy.at[i], zy_s.at[i])
+
+    @pl.when(own == 1)
+    def _():
+        for g in range(4):
+            all_sent(TB.at[g], tb_s.at[g])
+
+    all_sent(a_ref.at[:, 0:1536], sib_s)
     all_sent(LO, lo_s)
     for i in [0] + list(range(2, 8)):
         all_sent(w_ref, m_s.at[i])
@@ -398,12 +433,13 @@
         kernel,
         out_shape=jax.ShapeDtypeStruct((2, 64, 512), F32),
         in_specs=[
-            pl.BlockSpec(memory_space=pltpu.VMEM),
+            pl.BlockSpec(memory_space=pl.ANY),
             pl.BlockSpec(memory_space=pltpu.SMEM),
             pl.BlockSpec(memory_space=pltpu.SMEM),
         ],
         out_specs=pl.BlockSpec(memory_space=pltpu.VMEM),
         scratch_shapes=[
+            vmem((128, 4096), F32),
             vmem((4, 4, 1024, 128), F32),
             vmem((4, 1024, 128), F32),
             vmem((8, 8, 128), F32),
@@ -416,8 +452,9 @@
             vmem((2, 2, 3, 4, ROWS, 128), F32),
             vmem((2, 3, ROWS, 128), F32),
             vmem((2, 7, ROWS, 128), F32),
-            vmem((2, 4, 7, ROWS, 128), F32),
+            vmem((2, 3, 7, ROWS, 128), F32),
             vmem((128, 512), F32),
+            vmem((4, 128, 128), F32),
             dma((4, 4, 2, 4, 2)),
             dma((4, 2, 2, 4)),
             dma((4, 2)),
@@ -425,17 +462,20 @@
             dma((2, 2, 3)),
             dma((2, 3)),
             dma((2, 7)),
-            dma((2, 4, 7)),
+            dma((2, 3, 7)),
+            dma((4,)),
             dma,
             dma((2,)),
             dma((2,)),
             dma,
             dma,
             dma((8,)),
-            dma((2, 2)),
+            dma((2, 2, 3)),
+            dma((2, 3)),
             dma((2,)),
-            dma((2,)),
-            dma((2, 4)),
+            dma((2, 3)),
+            dma((4,)),
+            dma,
             dma,
         ],
         compiler_params=pltpu.CompilerParams(

time: 126 us -> 122 us (0.968)
  the two profiles are of different devices: /device:TPU:25 before, /device:TPU:17 now
where the time goes in v3:
time: 122 us
  Pallas kernels  120 us (98%)
  local copies, waits for them, and re-layouts  1.67 us (1%)
    pallas_call x1, Pallas kernels, per_device(): pl.pallas_call(kernel, out_shape=jax.ShapeDtypeStruct((2, 64, 512), F32),...  120 us

profile of v3, /device:TPU:17, one launch (start us, length us, event | category | flops | bytes accessed | tf_op | source)
XLA Modules:
  0.0 122.2 jit_solution(12143644991053204012)
XLA Ops:
  0.0 120.5 %sampled_gram.1 = f32[2,64,512]{2,1,0:T(8,128)} custom-call(f32[128,4096]{1,0:T(8,128)} %in_ref.1, s32[1,8]{1,0:T(1,128)} %mask_ref.1, f32[8]{0:T(128)} %rate_ref.1), custom_call_target="tpu_custom_call" | custom-call | tf_op jit(solution)/shard_map/sampled_gram/pallas_call | solution.py:432
  120.5 1.7 %copy.5 = f32[2,64,512]{2,1,0:T(8,128)} copy(f32[2,64,512]{2,1,0:T(8,128)} %sampled_gram.1) | data formatting | bytes 524288

commit v4 on v3

--- a/solution.py
+++ b/solution.py
@@ -14,28 +14,28 @@
 GROUPS = (((1, 1), (2, 1)), ((0, 1), (3, 1)), ((1, 2), (2, 2)), ((0, 2), (3, 2)))
 AHEAD = 1
 SCHEDULE = (
-    ("mul", (1, 0), (2, 0)), ("y", 2, 0, 0, 0), ("y", 1, 0, 1, 0), ("y", 1, 0, 0, 0), ("y", 2, 0, 1, 0),
-    ("mul", (0, 0), (3, 0)), ("pass", 0), ("z", 3, 0, 0), ("z", 0, 0, 0), ("z", 3, 0, 1),
-    ("mul", (1, 1), (2, 1)), ("y", 1, 1, 1, 0), ("y", 2, 1, 1, 0), ("y", 1, 1, 0, 0), ("y", 2, 1, 0, 0),
-    ("y", 2, 0, 0, 1), ("z", 0, 0, 1), ("y", 1, 0, 1, 1), ("pass", 1), ("z", 3, 0, 2), ("y", 1, 0, 0, 1),
-    ("z", 0, 0, 2), ("y", 2, 0, 1, 1), ("mul", (0, 1), (3, 1)), ("y", 1, 1, 1, 1), ("z", 3, 1, 0),
-    ("z", 0, 1, 0), ("z", 3, 0, 3), ("pass", 2), ("z", 0, 0, 3), ("y", 2, 1, 1, 1), ("z", 3, 1, 1),
-    ("y", 1, 1, 0, 1), ("y", 2, 1, 0, 1), ("z", 0, 1, 1), ("mul", (1, 2), (2, 2)), ("y", 1, 2, 1, 0),
-    ("y", 1, 0, 1, 2), ("z", 3, 0, 4), ("yz", 3, 0, 0), ("y", 2, 2, 0, 0), ("y", 2, 0, 0, 2), ("pass", 3),
-    ("y", 2, 2, 1, 0), ("z", 3, 1, 2), ("y", 1, 2, 0, 0), ("z", 0, 0, 4), ("yz", 0, 0, 0), ("y", 1, 0, 0, 2),
-    ("y", 2, 0, 1, 2), ("zy", 1, 0, 0), ("zy", 2, 0, 0), ("z", 0, 1, 2), ("y", 1, 1, 1, 2), ("z", 3, 1, 3),
-    ("y", 1, 1, 0, 2), ("zy", 1, 1, 0), ("y", 2, 1, 1, 2), ("yz", 3, 0, 1), ("mul", (0, 2), (3, 2)),
-    ("zy", 1, 0, 1), ("zy", 2, 0, 1), ("y", 1, 2, 1, 1), ("y", 2, 1, 0, 2), ("zy", 2, 1, 0), ("z", 0, 1, 3),
-    ("z", 0, 2, 0), ("z", 3, 2, 0), ("z", 3, 1, 4), ("yz", 3, 1, 0), ("y", 2, 2, 0, 1), ("zy", 1, 1, 1),
-    ("zy", 1, 0, 2), ("yz", 0, 0, 1), ("y", 2, 2, 1, 1), ("yz", 3, 0, 2), ("zy", 2, 0, 2), ("zy", 2, 1, 1),
-    ("z", 0, 1, 4), ("yz", 0, 1, 0), ("y", 1, 2, 0, 1), ("z", 0, 2, 1), ("yz", 3, 1, 1), ("z", 3, 2, 1),
-    ("yz", 0, 0, 2), ("y", 1, 2, 1, 2), ("yz", 0, 1, 1), ("zy", 1, 1, 2), ("zy", 1, 0, 3), ("y", 2, 2, 0, 2),
-    ("yz", 3, 1, 2), ("zy", 2, 0, 3), ("zy", 2, 1, 2), ("z", 0, 2, 2), ("y", 2, 2, 1, 2), ("zy", 2, 2, 0),
-    ("yz", 0, 1, 2), ("y", 1, 2, 0, 2), ("zy", 1, 2, 0), ("z", 3, 2, 2), ("zy", 1, 0, 4), ("zy", 1, 1, 3),
-    ("zy", 2, 0, 4), ("zy", 2, 1, 3), ("z", 0, 2, 3), ("zy", 2, 2, 1), ("zy", 1, 2, 1), ("z", 3, 2, 3),
-    ("zy", 1, 1, 4), ("zy", 2, 1, 4), ("turn",), ("z", 0, 2, 4), ("yz", 0, 2, 0), ("zy", 2, 2, 2),
-    ("zy", 1, 2, 2), ("z", 3, 2, 4), ("yz", 3, 2, 0), ("yz", 0, 2, 1), ("zy", 2, 2, 3), ("zy", 1, 2, 3),
-    ("yz", 3, 2, 1), ("yz", 0, 2, 2), ("yz", 3, 2, 2), ("zy", 2, 2, 4), ("zy", 1, 2, 4),
+    ("mul", (0, 0), (3, 0)), ("pass", 0), ("mul", (1, 0), (2, 0)), ("z", 0, 0, 0), ("y", 2, 0, 0, 0),
+    ("y", 1, 0, 1, 0), ("mul", (1, 1), (2, 1)), ("y", 2, 1, 1, 0), ("z", 0, 0, 1), ("y", 1, 1, 0, 0),
+    ("pass", 1), ("y", 2, 1, 0, 0), ("z", 3, 0, 0), ("z", 3, 0, 1), ("y", 1, 1, 1, 0), ("z", 0, 0, 2),
+    ("mul", (0, 1), (3, 1)), ("pass", 2), ("z", 0, 1, 0), ("z", 3, 1, 0), ("z", 3, 0, 2), ("y", 2, 0, 1, 0),
+    ("y", 1, 1, 0, 1), ("y", 1, 0, 1, 1), ("z", 0, 1, 1), ("mul", (1, 2), (2, 2)), ("z", 3, 1, 1),
+    ("y", 2, 2, 0, 0), ("z", 0, 0, 3), ("y", 2, 0, 0, 1), ("y", 1, 0, 0, 0), ("y", 2, 1, 0, 1),
+    ("y", 2, 2, 1, 0), ("pass", 3), ("y", 1, 2, 1, 0), ("z", 0, 1, 2), ("y", 1, 1, 1, 1), ("y", 1, 2, 0, 0),
+    ("y", 2, 1, 1, 1), ("y", 1, 1, 0, 2), ("z", 3, 0, 3), ("z", 3, 1, 2), ("mul", (0, 2), (3, 2)),
+    ("y", 2, 0, 1, 1), ("y", 2, 2, 1, 1), ("z", 3, 2, 0), ("y", 2, 2, 0, 1), ("z", 0, 2, 0), ("z", 3, 0, 4),
+    ("y", 1, 1, 1, 2), ("zy", 1, 1, 0), ("z", 0, 1, 3), ("y", 1, 0, 0, 1), ("z", 3, 1, 3), ("y", 1, 2, 1, 1),
+    ("z", 3, 2, 1), ("zy", 1, 1, 1), ("y", 2, 1, 0, 2), ("y", 2, 0, 0, 2), ("z", 0, 0, 4), ("z", 0, 2, 1),
+    ("y", 2, 1, 1, 2), ("yz", 0, 0, 0), ("y", 1, 0, 1, 2), ("zy", 2, 1, 0), ("y", 2, 0, 1, 2), ("z", 3, 2, 2),
+    ("z", 0, 1, 4), ("y", 1, 0, 0, 2), ("zy", 2, 0, 0), ("y", 2, 2, 0, 2), ("y", 1, 2, 0, 1), ("z", 0, 2, 2),
+    ("yz", 0, 0, 1), ("zy", 2, 1, 1), ("z", 3, 1, 4), ("yz", 3, 0, 0), ("zy", 1, 0, 0), ("zy", 1, 1, 2),
+    ("zy", 2, 1, 2), ("y", 2, 2, 1, 2), ("zy", 2, 2, 0), ("y", 1, 2, 1, 2), ("yz", 3, 1, 0), ("z", 3, 2, 3),
+    ("zy", 2, 2, 1), ("z", 0, 2, 3), ("yz", 3, 0, 1), ("zy", 2, 1, 3), ("y", 1, 2, 0, 2), ("zy", 2, 0, 1),
+    ("zy", 1, 1, 3), ("zy", 1, 2, 0), ("yz", 0, 1, 0), ("yz", 3, 1, 1), ("yz", 3, 1, 2), ("z", 3, 2, 4),
+    ("zy", 1, 1, 4), ("zy", 1, 2, 1), ("zy", 1, 0, 1), ("yz", 0, 1, 1), ("yz", 0, 1, 2), ("zy", 2, 1, 4),
+    ("yz", 3, 2, 0), ("z", 0, 2, 4), ("yz", 0, 2, 0), ("yz", 0, 0, 2), ("yz", 3, 2, 1), ("zy", 2, 0, 2),
+    ("zy", 2, 2, 2), ("turn",), ("zy", 1, 0, 2), ("zy", 1, 2, 2), ("zy", 2, 2, 3), ("zy", 1, 2, 3),
+    ("zy", 1, 0, 3), ("yz", 3, 2, 2), ("yz", 3, 0, 2), ("yz", 0, 2, 1), ("zy", 2, 2, 4), ("yz", 0, 2, 2),
+    ("zy", 2, 0, 3), ("zy", 2, 0, 4), ("zy", 1, 2, 4), ("zy", 1, 0, 4),
 )
 ROWS = 136
 F32 = jnp.float32

time: 122 us -> 118 us (0.967)
  the two profiles are of different devices: /device:TPU:17 before, /device:TPU:25 now
where the time goes in v4:
time: 118 us
  Pallas kernels  116 us (98%)
  local copies, waits for them, and re-layouts  1.67 us (1%)
    pallas_call x1, Pallas kernels, per_device(): pl.pallas_call(kernel, out_shape=jax.ShapeDtypeStruct((2, 64, 512), F32),...  116 us

profile of v4, /device:TPU:25, one launch (start us, length us, event | category | flops | bytes accessed | tf_op | source)
XLA Modules:
  0.0 117.6 jit_solution(11046960607150206361)
XLA Ops:
  0.0 115.9 %sampled_gram.1 = f32[2,64,512]{2,1,0:T(8,128)} custom-call(f32[128,4096]{1,0:T(8,128)} %in_ref.1, s32[1,8]{1,0:T(1,128)} %mask_ref.1, f32[8]{0:T(128)} %rate_ref.1), custom_call_target="tpu_custom_call" | custom-call | tf_op jit(solution)/shard_map/sampled_gram/pallas_call | solution.py:432
  115.9 1.7 %copy.5 = f32[2,64,512]{2,1,0:T(8,128)} copy(f32[2,64,512]{2,1,0:T(8,128)} %sampled_gram.1) | data formatting | bytes 524288

commit v5 on v4

--- a/solution.py
+++ b/solution.py
@@ -11,31 +11,31 @@
 MESH = pl.DeviceIdType.MESH
 OFFS = (2, 1, 3, 0)
 PLACE = {0: 0, 1: 1, 3: 2, 2: 3}
-GROUPS = (((1, 1), (2, 1)), ((0, 1), (3, 1)), ((1, 2), (2, 2)), ((0, 2), (3, 2)))
+GROUPS = (((1, 1), (2, 1)), ((0, 1), (1, 2)), ((2, 2), (3, 1)), ((0, 2), (3, 2)))
 AHEAD = 1
 SCHEDULE = (
-    ("mul", (0, 0), (3, 0)), ("pass", 0), ("mul", (1, 0), (2, 0)), ("z", 0, 0, 0), ("y", 2, 0, 0, 0),
-    ("y", 1, 0, 1, 0), ("mul", (1, 1), (2, 1)), ("y", 2, 1, 1, 0), ("z", 0, 0, 1), ("y", 1, 1, 0, 0),
-    ("pass", 1), ("y", 2, 1, 0, 0), ("z", 3, 0, 0), ("z", 3, 0, 1), ("y", 1, 1, 1, 0), ("z", 0, 0, 2),
-    ("mul", (0, 1), (3, 1)), ("pass", 2), ("z", 0, 1, 0), ("z", 3, 1, 0), ("z", 3, 0, 2), ("y", 2, 0, 1, 0),
-    ("y", 1, 1, 0, 1), ("y", 1, 0, 1, 1), ("z", 0, 1, 1), ("mul", (1, 2), (2, 2)), ("z", 3, 1, 1),
-    ("y", 2, 2, 0, 0), ("z", 0, 0, 3), ("y", 2, 0, 0, 1), ("y", 1, 0, 0, 0), ("y", 2, 1, 0, 1),
-    ("y", 2, 2, 1, 0), ("pass", 3), ("y", 1, 2, 1, 0), ("z", 0, 1, 2), ("y", 1, 1, 1, 1), ("y", 1, 2, 0, 0),
-    ("y", 2, 1, 1, 1), ("y", 1, 1, 0, 2), ("z", 3, 0, 3), ("z", 3, 1, 2), ("mul", (0, 2), (3, 2)),
-    ("y", 2, 0, 1, 1), ("y", 2, 2, 1, 1), ("z", 3, 2, 0), ("y", 2, 2, 0, 1), ("z", 0, 2, 0), ("z", 3, 0, 4),
-    ("y", 1, 1, 1, 2), ("zy", 1, 1, 0), ("z", 0, 1, 3), ("y", 1, 0, 0, 1), ("z", 3, 1, 3), ("y", 1, 2, 1, 1),
-    ("z", 3, 2, 1), ("zy", 1, 1, 1), ("y", 2, 1, 0, 2), ("y", 2, 0, 0, 2), ("z", 0, 0, 4), ("z", 0, 2, 1),
-    ("y", 2, 1, 1, 2), ("yz", 0, 0, 0), ("y", 1, 0, 1, 2), ("zy", 2, 1, 0), ("y", 2, 0, 1, 2), ("z", 3, 2, 2),
-    ("z", 0, 1, 4), ("y", 1, 0, 0, 2), ("zy", 2, 0, 0), ("y", 2, 2, 0, 2), ("y", 1, 2, 0, 1), ("z", 0, 2, 2),
-    ("yz", 0, 0, 1), ("zy", 2, 1, 1), ("z", 3, 1, 4), ("yz", 3, 0, 0), ("zy", 1, 0, 0), ("zy", 1, 1, 2),
-    ("zy", 2, 1, 2), ("y", 2, 2, 1, 2), ("zy", 2, 2, 0), ("y", 1, 2, 1, 2), ("yz", 3, 1, 0), ("z", 3, 2, 3),
-    ("zy", 2, 2, 1), ("z", 0, 2, 3), ("yz", 3, 0, 1), ("zy", 2, 1, 3), ("y", 1, 2, 0, 2), ("zy", 2, 0, 1),
-    ("zy", 1, 1, 3), ("zy", 1, 2, 0), ("yz", 0, 1, 0), ("yz", 3, 1, 1), ("yz", 3, 1, 2), ("z", 3, 2, 4),
-    ("zy", 1, 1, 4), ("zy", 1, 2, 1), ("zy", 1, 0, 1), ("yz", 0, 1, 1), ("yz", 0, 1, 2), ("zy", 2, 1, 4),
-    ("yz", 3, 2, 0), ("z", 0, 2, 4), ("yz", 0, 2, 0), ("yz", 0, 0, 2), ("yz", 3, 2, 1), ("zy", 2, 0, 2),
-    ("zy", 2, 2, 2), ("turn",), ("zy", 1, 0, 2), ("zy", 1, 2, 2), ("zy", 2, 2, 3), ("zy", 1, 2, 3),
-    ("zy", 1, 0, 3), ("yz", 3, 2, 2), ("yz", 3, 0, 2), ("yz", 0, 2, 1), ("zy", 2, 2, 4), ("yz", 0, 2, 2),
-    ("zy", 2, 0, 3), ("zy", 2, 0, 4), ("zy", 1, 2, 4), ("zy", 1, 0, 4),
+    ("mul", (0, 0), (3, 0)), ("z", 3, 0, 0), ("pass", 0), ("mul", (1, 0), (2, 0)), ("z", 0, 0, 0),
+    ("y", 1, 0, 1, 0), ("y", 1, 0, 0, 0), ("z", 3, 0, 1), ("mul", (1, 1), (2, 1)), ("y", 1, 1, 1, 0),
+    ("y", 2, 0, 0, 0), ("z", 3, 0, 2), ("y", 2, 1, 0, 0), ("z", 0, 0, 1), ("y", 2, 1, 1, 0), ("pass", 1),
+    ("y", 1, 0, 1, 1), ("y", 1, 1, 0, 0), ("mul", (0, 1), (1, 2)), ("y", 1, 2, 1, 0), ("z", 0, 1, 0),
+    ("z", 0, 0, 2), ("pass", 2), ("y", 2, 0, 1, 0), ("y", 1, 2, 0, 0), ("y", 2, 1, 0, 1), ("z", 0, 1, 1),
+    ("mul", (2, 2), (3, 1)), ("z", 3, 1, 0), ("z", 3, 0, 3), ("y", 1, 0, 1, 2), ("y", 2, 0, 0, 1),
+    ("pass", 3), ("y", 1, 2, 1, 1), ("y", 2, 2, 1, 0), ("z", 0, 0, 3), ("y", 1, 0, 0, 1), ("y", 1, 1, 1, 1),
+    ("y", 1, 1, 0, 1), ("y", 2, 0, 1, 1), ("z", 3, 1, 1), ("z", 0, 1, 2), ("mul", (0, 2), (3, 2)),
+    ("z", 0, 2, 0), ("z", 3, 0, 4), ("z", 0, 0, 4), ("z", 3, 2, 0), ("y", 2, 2, 0, 0), ("y", 1, 2, 0, 1),
+    ("y", 2, 1, 1, 1), ("y", 2, 0, 0, 2), ("z", 3, 1, 2), ("y", 2, 1, 0, 2), ("z", 0, 2, 1), ("z", 3, 2, 1),
+    ("y", 1, 1, 0, 2), ("y", 1, 1, 1, 2), ("zy", 1, 1, 0), ("y", 2, 1, 1, 2), ("z", 0, 1, 3), ("z", 3, 1, 3),
+    ("y", 1, 0, 0, 2), ("y", 1, 2, 1, 2), ("zy", 1, 0, 0), ("zy", 2, 1, 0), ("y", 1, 2, 0, 2),
+    ("y", 2, 2, 1, 1), ("zy", 1, 1, 1), ("y", 2, 2, 0, 1), ("yz", 0, 0, 0), ("z", 3, 2, 2), ("zy", 1, 2, 0),
+    ("z", 0, 1, 4), ("yz", 0, 1, 0), ("zy", 2, 1, 1), ("z", 0, 2, 2), ("zy", 1, 1, 2), ("y", 2, 2, 1, 2),
+    ("y", 2, 0, 1, 2), ("zy", 1, 0, 1), ("yz", 3, 0, 0), ("z", 3, 1, 4), ("yz", 3, 1, 0), ("zy", 2, 1, 2),
+    ("z", 3, 2, 3), ("zy", 1, 2, 1), ("zy", 1, 1, 3), ("yz", 3, 0, 1), ("zy", 2, 0, 0), ("yz", 0, 0, 1),
+    ("zy", 1, 0, 2), ("yz", 3, 1, 1), ("yz", 0, 1, 1), ("z", 0, 2, 3), ("yz", 3, 1, 2), ("y", 2, 2, 0, 2),
+    ("zy", 2, 2, 0), ("zy", 2, 1, 3), ("zy", 2, 0, 1), ("z", 0, 2, 4), ("zy", 2, 2, 1), ("yz", 0, 2, 0),
+    ("zy", 1, 2, 2), ("zy", 1, 1, 4), ("zy", 2, 2, 2), ("yz", 0, 1, 2), ("yz", 0, 0, 2), ("yz", 0, 2, 1),
+    ("yz", 0, 2, 2), ("z", 3, 2, 4), ("zy", 1, 2, 3), ("zy", 2, 2, 3), ("yz", 3, 2, 0), ("yz", 3, 2, 1),
+    ("zy", 2, 1, 4), ("zy", 2, 0, 2), ("zy", 1, 2, 4), ("zy", 1, 0, 3), ("zy", 2, 0, 3), ("zy", 1, 0, 4),
+    ("yz", 3, 0, 2), ("zy", 2, 0, 4), ("turn",), ("yz", 3, 2, 2), ("zy", 2, 2, 4),
 )
 ROWS = 136
 F32 = jnp.float32

time: 118 us -> 118 us (level)
  no operation moved by 1% of the time
where the time goes in v5:
time: 118 us
  Pallas kernels  116 us (98%)
  local copies, waits for them, and re-layouts  1.67 us (1%)
    pallas_call x1, Pallas kernels, per_device(): pl.pallas_call(kernel, out_shape=jax.ShapeDtypeStruct((2, 64, 512), F32),...  116 us

profile of v5, /device:TPU:25, one launch (start us, length us, event | category | flops | bytes accessed | tf_op | source)
XLA Modules:
  0.0 118.1 jit_solution(3703805716999755082)
XLA Ops:
  0.0 116.5 %sampled_gram.1 = f32[2,64,512]{2,1,0:T(8,128)} custom-call(f32[128,4096]{1,0:T(8,128)} %in_ref.1, s32[1,8]{1,0:T(1,128)} %mask_ref.1, f32[8]{0:T(128)} %rate_ref.1), custom_call_target="tpu_custom_call" | custom-call | tf_op jit(solution)/shard_map/sampled_gram/pallas_call | solution.py:432
  116.5 1.7 %copy.5 = f32[2,64,512]{2,1,0:T(8,128)} copy(f32[2,64,512]{2,1,0:T(8,128)} %sampled_gram.1) | data formatting | bytes 524288
